TPU v7x, 512 devices: a whole 4x4x16 slice. The times are simulated.
512 devices in a mesh: dom: 16 (over x, y_lo, core), shard: 32 (over y_hi, z).
Axes of the slice: x: 4, y: 4 (y_hi: 2, y_lo: 2; y = y_hi * 2 + y_lo), z: 16, core: 2. Of those that a mesh axis runs over, the one named last changes fastest.
Arguments:
- embeddings: float32 [32768, 400], P(('dom', 'shard')), may hold values from -3 to 3
- row_accum: float32 [32768], P(('dom', 'shard')), may hold values from 0.01 to 1
- relations: bfloat16 [2560, 400], replicated, may hold values from -3 to 3
- relation_accum: float32 [2560], P(('dom', 'shard')), may hold values from 0.01 to 1
- request_rows: int32 [2, 16384, 2, 16], P(None, ('dom', 'shard')), may hold values from 0 to 63
- head_slots: int32 [2, 65536], P(None, ('dom', 'shard')), may hold values from 0 to 511
- tail_slots: int32 [2, 65536], P(None, ('dom', 'shard')), may hold values from 0 to 511
- relation_ids: int32 [2, 65536], P(None, ('dom', 'shard')), may hold values from 0 to 2559
- own_negatives: int32 [2, 262144], P(None, ('dom', 'shard')), may hold values from 0 to 511
- far_negatives: int32 [2, 262144], P(None, ('dom', 'shard')), may hold values from 0 to 511
Outputs:
- new_embeddings: float32 [32768, 400], P(('dom', 'shard'))
- new_accum: float32 [32768], P(('dom', 'shard'))
- relation_step: float32 [2560, 400], P(('dom', 'shard'))
- new_relation_accum: float32 [2560], P(('dom', 'shard'))
Inputs may be any that keep to these rules, and one draw needn't show every extreme that they name: `request_rows`: local row numbers within the owner's 64 rows. `head_slots`: slots of the 512 own-side touched rows. `tail_slots`: slots of the 512 partner-side touched rows. `own_negatives`: slots of the 512 own-side touched rows. `far_negatives`: slots of the 512 partner-side touched rows.
All inputs are finite; a program needn't handle non-finite values.
Results may differ from a plain program's by a relative error of at most 0.0049.
Values may be sent and summed in bfloat16 or wider, within the bound.
A program may use at most 64 MiB of HBM per device.

v0:
```python
import jax
import jax.numpy as jnp
from jax import lax
from jax.sharding import PartitionSpec as P

LEARN_RATE = 0.1
BF = jnp.bfloat16
F32 = jnp.float32


def partner(value, axis, distance):
    mask = 2**distance
    pairs = [(source, source ^ mask) for source in range(lax.axis_size(axis))]
    return lax.ppermute(value, axis, pairs)


def mm(a, b, ca, cb):
    return lax.dot_general(a, b, (((ca,), (cb,)), ((), ())), preferred_element_type=F32)


def one_hot(ids, n):
    return (ids[:, None] == jnp.arange(n, dtype=ids.dtype)[None, :]).astype(BF)


def split_mm(a, b, ca, cb):
    hi = b.astype(BF)
    lo = (b - hi.astype(F32)).astype(BF)
    return mm(a, hi, ca, cb) + mm(a, lo, ca, cb)


def edge_terms(own, far, head_slots, tail_slots, rel_vec, own_neg, far_neg):
    touch = own.shape[0]
    neg = own_neg.shape[0]
    head_hot = one_hot(head_slots, touch)
    tail_hot = one_hot(tail_slots, touch)
    head_vec = mm(head_hot, own, 1, 0)
    tail_vec = mm(tail_hot, far, 1, 0)
    slots = jnp.arange(touch, dtype=own_neg.dtype)
    own_count = jnp.sum((own_neg[:, None] == slots[None, :]).astype(F32), axis=0)
    far_count = jnp.sum((far_neg[:, None] == slots[None, :]).astype(F32), axis=0)
    positive = jnp.sum(head_vec * rel_vec * tail_vec, axis=-1)
    query_tail = (head_vec * rel_vec).astype(BF)
    query_head = (tail_vec * rel_vec).astype(BF)
    score_tail = mm(query_tail, far, 1, 1)
    score_head = mm(query_head, own, 1, 1)
    weight_tail = (jax.nn.sigmoid(score_tail) * (far_count / neg)).astype(BF)
    weight_head = (jax.nn.sigmoid(score_head) * (own_count / neg)).astype(BF)
    back_tail = mm(weight_tail, far, 1, 0)
    back_head = mm(weight_head, own, 1, 0)
    coeff = -jax.nn.sigmoid(-positive)[:, None]
    grad_head = rel_vec * (coeff * tail_vec + back_tail)
    grad_tail = rel_vec * (coeff * head_vec + back_head)
    grad_rel = coeff * head_vec * tail_vec + head_vec * back_tail + tail_vec * back_head
    own_grad = split_mm(head_hot, grad_head, 0, 0) + mm(weight_head, query_head, 0, 0)
    far_grad = split_mm(tail_hot, grad_tail, 0, 0) + mm(weight_tail, query_tail, 0, 0)
    return (own_grad.astype(BF), far_grad.astype(BF), grad_rel)


def body(
    embeddings,
    row_accum,
    relations,
    relation_accum,
    request_rows,
    head_slots,
    tail_slots,
    relation_ids,
    own_negatives,
    far_negatives,
):
    rows, width = embeddings.shape
    shards = lax.axis_size("shard")
    slot_count = request_rows.shape[-1]
    touch = shards * slot_count
    rounds = request_rows.shape[0]
    emb = embeddings
    accum = row_accum
    rel_rows = []
    all_rel = relations[relation_ids.reshape(-1)].astype(F32).reshape(rounds, -1, width)
    for r in range(rounds):
        lowered = emb.astype(BF)
        ids = request_rows[r].reshape(-1)
        hot = one_hot(ids, rows)
        served = mm(hot, lowered, 1, 0).astype(BF).reshape(shards, 2, slot_count, width)
        received = lax.all_to_all(served, "shard", split_axis=0, concat_axis=0, tiled=True)
        own = received[:, 0].reshape(touch, width)
        far = partner(received[:, 1].reshape(touch, width), "dom", r)
        own_grad, far_grad, grad_rel = edge_terms(
            own, far, head_slots[r], tail_slots[r], all_rel[r], own_negatives[r], far_negatives[r]
        )
        rel_rows.append(grad_rel.astype(BF))
        far_back = partner(far_grad, "dom", r)
        outgoing = jnp.stack(
            [
                own_grad.reshape(shards, slot_count, width),
                far_back.reshape(shards, slot_count, width),
            ],
            axis=1,
        )
        returned = lax.all_to_all(outgoing, "shard", split_axis=0, concat_axis=0, tiled=True)
        row_grad = mm(hot, returned.reshape(-1, width), 0, 0)
        accum = accum + jnp.mean(row_grad * row_grad, axis=-1)
        emb = emb - LEARN_RATE * row_grad / jnp.sqrt(accum)[:, None]
    mine = jnp.concatenate(rel_rows, axis=0)
    ids = lax.all_gather(relation_ids.reshape(-1), "dom", tiled=True)
    group_rows = lax.all_gather(mine, "dom", tiled=True)
    per_group = relations.shape[0] // lax.axis_size("dom")
    local = ids - lax.axis_index("dom").astype(ids.dtype) * per_group
    dense = mm(one_hot(local, per_group), group_rows, 0, 0)
    pieces = dense.reshape(shards, per_group // shards, width)
    pieces = lax.all_to_all(pieces, "shard", split_axis=0, concat_axis=0, tiled=True)
    own_share = jnp.sum(pieces, axis=0)
    new_relation_accum = relation_accum + jnp.mean(own_share * own_share, axis=-1)
    relation_step = -LEARN_RATE * own_share / jnp.sqrt(new_relation_accum)[:, None]
    return (emb, accum, relation_step, new_relation_accum)


def solution(mesh):
    both = ("dom", "shard")
    return jax.shard_map(
        body,
        mesh=mesh,
        in_specs=(P(both, None), P(both), P(), P(both), P(None, both, None, None))
        + (P(None, both),) * 5,
        out_specs=(P(both, None), P(both), P(both, None), P(both)),
        check_vma=False,
    )
```

profile of v0, /device:TPU:2, one launch (start us, length us, event | category | flops | bytes accessed | tf_op | source)
XLA Modules:
  0.0 351.7 jit_solution(11925494591055917611)
XLA Ops:
  7.2 0.7 fusion.69
  8.1 1.5 convolution_convert_fusion.1
  9.6 1.3 copy.43
  10.9 18.2 %all-to-all-start = ((bf16[32,2,16,400]{3,2,1,0:T(8,128)(2,1)}), bf16[32,2,16,400]{3,2,1,0:T(8,128)(2,1)}, u32[]{:S(2)}, u32[]{:S(2)}) async-start(bf16[32,2,16,400]{3,2,1,0:T(8,128)(2,1)} %bitcast.3), calls=%async_computation | async-start | bytes 2097152 | tf_op jit(solution)/shard_map/all_to_all | solution.py:85
  29.1 2.9 copy.41
  32.1 1.2 gather_fusion
  33.9 47.7 %all-to-all-done = bf16[32,2,16,400]{3,2,1,0:T(8,128)(2,1)} async-done(((bf16[32,2,16,400]{3,2,1,0:T(8,128)(2,1)}), bf16[32,2,16,400]{3,2,1,0:T(8,128)(2,1)}, u32[]{:S(2)}, u32[]{:S(2)}) %all-to-all-start) | async-done | bytes 819232 | tf_op jit(solution)/shard_map/all_to_all | solution.py:85
  81.5 1.3 fusion.68
  82.8 1.9 collective-permute-start
  84.8 1.8 collective-permute-done
  89.8 2.0 collective-permute-start.1
  93.8 1.1 copy.46
  94.8 7.9 %all-to-all-start.1 = ((bf16[32,2,16,400]{3,2,1,0:T(8,128)(2,1)}), bf16[32,2,16,400]{3,2,1,0:T(8,128)(2,1)S(1)}, u32[]{:S(2)}, u32[]{:S(2)}) async-start(bf16[32,2,16,400]{3,2,1,0:T(8,128)(2,1)} %copy.46), calls=%async_computation.1 | async-start | bytes 2097152 | tf_op jit(solution)/shard_map/all_to_all | solution.py:100
  103.0 52.4 %all-to-all-done.1 = bf16[32,2,16,400]{3,2,1,0:T(8,128)(2,1)S(1)} async-done(((bf16[32,2,16,400]{3,2,1,0:T(8,128)(2,1)}), bf16[32,2,16,400]{3,2,1,0:T(8,128)(2,1)S(1)}, u32[]{:S(2)}, u32[]{:S(2)}) %all-to-all-start.1) | async-done | bytes 819232 | tf_op jit(solution)/shard_map/all_to_all | solution.py:100
  156.5 1.3 copy.48
  157.8 8.1 %all-to-all-start.2 = ((bf16[32,2,16,400]{3,2,1,0:T(8,128)(2,1)}), bf16[32,2,16,400]{3,2,1,0:T(8,128)(2,1)S(1)}, u32[]{:S(2)}, u32[]{:S(2)}) async-start(bf16[32,2,16,400]{3,2,1,0:T(8,128)(2,1)} %bitcast.13), calls=%async_computation.2 | async-start | bytes 2097152 | tf_op jit(solution)/shard_map/all_to_all | solution.py:85
  166.3 51.9 %all-to-all-done.2 = bf16[32,2,16,400]{3,2,1,0:T(8,128)(2,1)S(1)} async-done(((bf16[32,2,16,400]{3,2,1,0:T(8,128)(2,1)}), bf16[32,2,16,400]{3,2,1,0:T(8,128)(2,1)S(1)}, u32[]{:S(2)}, u32[]{:S(2)}) %all-to-all-start.2) | async-done | bytes 819232 | tf_op jit(solution)/shard_map/all_to_all | solution.py:85
  218.4 2.6 collective-permute-start.2
  221.0 11.5 %collective-permute-done.2 = bf16[512,400]{1,0:T(8,128)(2,1)S(1)} collective-permute-done((bf16[512,400]{1,0:T(8,128)(2,1)S(1)}, bf16[512,400]{1,0:T(8,128)(2,1)S(1)}, u32[]{:S(2)}, u32[]{:S(2)}) %collective-permute-start.2) | collective-permute-done | bytes 409632 | tf_op jit(solution)/shard_map/ppermute | solution.py:14
  236.3 2.8 collective-permute-start.3
  240.3 6.8 %collective-permute-done.3 = bf16[512,400]{0,1:T(8,128)(2,1)S(1)} collective-permute-done((bf16[512,400]{0,1:T(8,128)(2,1)S(1)}, bf16[512,400]{0,1:T(8,128)(2,1)S(1)}, u32[]{:S(2)}, u32[]{:S(2)}) %collective-permute-start.3) | collective-permute-done | bytes 409632 | tf_op jit(solution)/shard_map/ppermute | solution.py:14
  247.4 1.1 copy.51
  248.5 11.0 %all-to-all-start.3 = ((bf16[32,2,16,400]{3,2,1,0:T(8,128)(2,1)}), bf16[32,2,16,400]{3,2,1,0:T(8,128)(2,1)S(1)}, u32[]{:S(2)}, u32[]{:S(2)}) async-start(bf16[32,2,16,400]{3,2,1,0:T(8,128)(2,1)} %copy.51), calls=%async_computation.3 | async-start | bytes 2097152 | tf_op jit(solution)/shard_map/all_to_all | solution.py:100
  259.5 16.7 %all-gather = s32[16,1,256]{2,1,0:T(1,128)S(1)} all-gather(s32[1,1,256]{2,1,0:T(1,128)S(1)} %bitcast.82), channel_id=1, replica_groups=mesh['dom'=16,'shard'=32] {'dom'}, dimensions={0}, use_global_device_ids=true | all-gather | bytes 17408 | tf_op jit(solution)/shard_map/all_gather | solution.py:105
  276.2 5.0 %all-gather.3.cloned.1.call-done = bf16[4096,400]{0,1:T(8,128)(2,1)} async-done(((bf16[256,400]{0,1:T(8,128)(2,1)}), bf16[4096,400]{0,1:T(8,128)(2,1)}) %all-gather.3.cloned.1.call-update) | async-done | bytes 3276816 | tf_op jit(solution)/shard_map/all_gather | solution.py:106
  281.2 3.0 fusion
  284.4 1.3 reshape.122
  285.6 25.2 %all-to-all-done.3 = bf16[32,2,16,400]{3,2,1,0:T(8,128)(2,1)S(1)} async-done(((bf16[32,2,16,400]{3,2,1,0:T(8,128)(2,1)}), bf16[32,2,16,400]{3,2,1,0:T(8,128)(2,1)S(1)}, u32[]{:S(2)}, u32[]{:S(2)}) %all-to-all-start.3) | async-done | bytes 819232 | tf_op jit(solution)/shard_map/all_to_all | solution.py:100
  310.9 7.4 %all-to-all-start.4 = ((f32[32,1,2000]{2,1,0:T(1,128)}), f32[32,1,2000]{2,1,0:T(1,128)S(1)}, u32[]{:S(2)}, u32[]{:S(2)}) async-start(f32[32,1,2000]{2,1,0:T(1,128)} %reshape.122), calls=%async_computation.4 | async-start | bytes 524288 | tf_op jit(solution)/shard_map/all_to_all | solution.py:111
  319.4 0.8 divide_subtract_fusion
  320.2 21.2 %all-to-all-done.4 = f32[32,1,2000]{2,1,0:T(1,128)S(1)} async-done(((f32[32,1,2000]{2,1,0:T(1,128)}), f32[32,1,2000]{2,1,0:T(1,128)S(1)}, u32[]{:S(2)}, u32[]{:S(2)}) %all-to-all-start.4) | async-done | bytes 256032 | tf_op jit(solution)/shard_map/all_to_all | solution.py:111
  341.9 1.3 reduce
  (86 shorter events, 16.2 us)
Async XLA Ops:
  10.9 70.7 %all-to-all-start = ((bf16[32,2,16,400]{3,2,1,0:T(8,128)(2,1)}), bf16[32,2,16,400]{3,2,1,0:T(8,128)(2,1)}, u32[]{:S(2)}, u32[]{:S(2)}) async-start(bf16[32,2,16,400]{3,2,1,0:T(8,128)(2,1)} %bitcast.3), calls=%async_computation | async-start | bytes 2097152 | tf_op jit(solution)/shard_map/all_to_all | solution.py:85
  29.1 2.9 copy-start.1
  32.0 1.4 copy-start.2
  32.0 1.6 copy-start.3
  32.0 1.8 copy-start.4
  32.1 52.7 %copy-start.5 = (s32[2,128]{1,0:T(2,128)S(1)}, s32[2,128]{1,0:T(2,128)}, u32[]{:S(2)}) copy-start(s32[2,128]{1,0:T(2,128)} %param.15) | copy-start | bytes 3076
  82.8 3.8 %collective-permute-start = (bf16[512,400]{1,0:T(8,128)(2,1)S(1)}, bf16[512,400]{1,0:T(8,128)(2,1)S(1)}, u32[]{:S(2)}, u32[]{:S(2)}) collective-permute-start(bf16[512,400]{1,0:T(8,128)(2,1)S(1)} %bitcast.73), channel_id=1, source_target_pairs={{0,32},{32,0},{64,96},{96,64},{128,160},{160,128},{192,224},{224,1... | collective-permute-start | bytes 1228808 | tf_op jit(solution)/shard_map/ppermute | solution.py:14
  89.8 3.6 %collective-permute-start.1 = (bf16[512,400]{0,1:T(8,128)(2,1)S(1)}, bf16[512,400]{0,1:T(8,128)(2,1)S(1)}, u32[]{:S(2)}, u32[]{:S(2)}) collective-permute-start(bf16[512,400]{0,1:T(8,128)(2,1)S(1)} %fusion.3), channel_id=1, source_target_pairs={{0,32},{32,0},{64,96},{96,64},{128,160},{160,128},{192,224},{224,1... | collective-permute-start | bytes 1228808 | tf_op jit(solution)/shard_map/ppermute | solution.py:14
  93.7 62.1 %copy-start.6 = (f32[64]{0:T(128)S(1)}, f32[64]{0:T(128)}, u32[]{:S(2)}) copy-start(f32[64]{0:T(128)} %param.11) | copy-start | bytes 772
  93.8 62.2 %copy-start = (f32[64,400]{1,0:T(8,128)S(1)}, f32[64,400]{1,0:T(8,128)}, u32[]{:S(2)}) copy-start(f32[64,400]{1,0:T(8,128)} %param.10) | copy-start | bytes 307204
  94.8 60.5 %all-to-all-start.1 = ((bf16[32,2,16,400]{3,2,1,0:T(8,128)(2,1)}), bf16[32,2,16,400]{3,2,1,0:T(8,128)(2,1)S(1)}, u32[]{:S(2)}, u32[]{:S(2)}) async-start(bf16[32,2,16,400]{3,2,1,0:T(8,128)(2,1)} %copy.46), calls=%async_computation.1 | async-start | bytes 2097152 | tf_op jit(solution)/shard_map/all_to_all | solution.py:100
  157.8 60.5 %all-to-all-start.2 = ((bf16[32,2,16,400]{3,2,1,0:T(8,128)(2,1)}), bf16[32,2,16,400]{3,2,1,0:T(8,128)(2,1)S(1)}, u32[]{:S(2)}, u32[]{:S(2)}) async-start(bf16[32,2,16,400]{3,2,1,0:T(8,128)(2,1)} %bitcast.13), calls=%async_computation.2 | async-start | bytes 2097152 | tf_op jit(solution)/shard_map/all_to_all | solution.py:85
  165.9 115.3 %all-gather.3.cloned.1.call-start = ((), (), s32[]{:S(2)}) async-start(), calls=%async_computation.5 | async-start | bytes 3481600 | tf_op jit(solution)/shard_map/all_gather | solution.py:106
  218.4 14.1 %collective-permute-start.2 = (bf16[512,400]{1,0:T(8,128)(2,1)S(1)}, bf16[512,400]{1,0:T(8,128)(2,1)S(1)}, u32[]{:S(2)}, u32[]{:S(2)}) collective-permute-start(bf16[512,400]{1,0:T(8,128)(2,1)S(1)} %bitcast.74), channel_id=1, source_target_pairs={{0,64},{32,96},{64,0},{96,32},{128,192},{160,224},{192,128},{224,1... | collective-permute-start | bytes 1228808 | tf_op jit(solution)/shard_map/ppermute | solution.py:14
  236.3 10.7 %collective-permute-start.3 = (bf16[512,400]{0,1:T(8,128)(2,1)S(1)}, bf16[512,400]{0,1:T(8,128)(2,1)S(1)}, u32[]{:S(2)}, u32[]{:S(2)}) collective-permute-start(bf16[512,400]{0,1:T(8,128)(2,1)S(1)} %fusion.5), channel_id=1, source_target_pairs={{0,64},{32,96},{64,0},{96,32},{128,192},{160,224},{192,128},{224,1... | collective-permute-start | bytes 1228808 | tf_op jit(solution)/shard_map/ppermute | solution.py:14
  248.5 62.3 %all-to-all-start.3 = ((bf16[32,2,16,400]{3,2,1,0:T(8,128)(2,1)}), bf16[32,2,16,400]{3,2,1,0:T(8,128)(2,1)S(1)}, u32[]{:S(2)}, u32[]{:S(2)}) async-start(bf16[32,2,16,400]{3,2,1,0:T(8,128)(2,1)} %copy.51), calls=%async_computation.3 | async-start | bytes 2097152 | tf_op jit(solution)/shard_map/all_to_all | solution.py:100
  284.4 59.3 %copy-start.7 = (f32[5]{0:T(128)S(1)}, f32[5]{0:T(128)}, u32[]{:S(2)}) copy-start(f32[5]{0:T(128)} %param.13) | copy-start | bytes 64
  310.9 30.5 %all-to-all-start.4 = ((f32[32,1,2000]{2,1,0:T(1,128)}), f32[32,1,2000]{2,1,0:T(1,128)S(1)}, u32[]{:S(2)}, u32[]{:S(2)}) async-start(f32[32,1,2000]{2,1,0:T(1,128)} %reshape.122), calls=%async_computation.4 | async-start | bytes 524288 | tf_op jit(solution)/shard_map/all_to_all | solution.py:111
Sparse Core Ops, SparseCore 0:
  235.5 45.7 all-gather.2
where the time goes:
time: 353 us; the launch traced here: 352 us
  waiting for transfers between devices  224 us (63%)
  starting transfers between devices  62.1 us (18%)
  blocking collectives  16.7 us (5%)
  between operations  14.6 us (4%)
  local copies, waits for them, and re-layouts  14.4 us (4%)
  matrix products  14.3 us (4%)
  other arithmetic  5.68 us (2%)
    all_to_all x2, waiting for transfers between devices, body(): lax.all_to_all(served, 'shard', split_axis=0, concat_axis=0, tiled=True)  99.6 us
    all_to_all x2, waiting for transfers between devices, body(): lax.all_to_all(outgoing, 'shard', split_axis=0, concat_axis=0, tiled=True)  77.6 us
    all_to_all x2, starting transfers between devices, body(): lax.all_to_all(served, 'shard', split_axis=0, concat_axis=0, tiled=True)  26.4 us
    all_to_all x1, waiting for transfers between devices, body(): lax.all_to_all(pieces, 'shard', split_axis=0, concat_axis=0, tiled=True)  21.2 us
    ppermute x4, waiting for transfers between devices, partner(): return lax.ppermute(value, axis, pairs)  20.5 us
    all_to_all x2, starting transfers between devices, body(): lax.all_to_all(outgoing, 'shard', split_axis=0, concat_axis=0, tiled=True)  19 us
    all_gather x1, blocking collectives, body(): ids = lax.all_gather(relation_ids.reshape(-1), 'dom', tiled=True)  16.7 us
    dot_general x29, matrix products, mm(): lax.dot_general(a, b, (((ca,), (cb,)), ((), ())), preferred_element_type=...  14.3 us
  transfers between devices with their start and end apart: 10, of which 10 were waited for; matrix products, arithmetic and copies ran while one was open for 5% of the time, Pallas kernels for 0%

commit v1 on v0

--- a/solution.py
+++ b/solution.py
@@ -102,7 +102,11 @@
         accum = accum + jnp.mean(row_grad * row_grad, axis=-1)
         emb = emb - LEARN_RATE * row_grad / jnp.sqrt(accum)[:, None]
     mine = jnp.concatenate(rel_rows, axis=0)
-    ids = lax.all_gather(relation_ids.reshape(-1), "dom", tiled=True)
+    own_2 = relation_ids.reshape(-1)
+    peers = lax.axis_size("dom")
+    blocks = jnp.stack([own_2 for _ in range(peers)])
+    blocks = lax.all_to_all(blocks, "dom", split_axis=0, concat_axis=0)
+    ids = jnp.concatenate(blocks, axis=0)
     group_rows = lax.all_gather(mine, "dom", tiled=True)
     per_group = relations.shape[0] // lax.axis_size("dom")
     local = ids - lax.axis_index("dom").astype(ids.dtype) * per_group

time: 353 us -> 366 us (1.037)
  the two profiles are of different devices: /device:TPU:2 before, /device:TPU:14 now
where the time goes in v1:
time: 366 us; the launch traced here: 365 us
  waiting for transfers between devices  250 us (68%)
  starting transfers between devices  65.4 us (18%)
  local copies, waits for them, and re-layouts  15 us (4%)
  between operations  14.6 us (4%)
  matrix products  14.3 us (4%)
  other arithmetic  5.69 us (2%)
    all_to_all x2, waiting for transfers between devices, body(): lax.all_to_all(served, 'shard', split_axis=0, concat_axis=0, tiled=True)  99.6 us
    all_to_all x2, waiting for transfers between devices, body(): lax.all_to_all(outgoing, 'shard', split_axis=0, concat_axis=0, tiled=True)  91.8 us
    ppermute x4, waiting for transfers between devices, partner(): return lax.ppermute(value, axis, pairs)  29.6 us
    all_to_all x2, starting transfers between devices, body(): lax.all_to_all(served, 'shard', split_axis=0, concat_axis=0, tiled=True)  25.5 us
    all_to_all x1, waiting for transfers between devices, body(): lax.all_to_all(pieces, 'shard', split_axis=0, concat_axis=0, tiled=True)  21.2 us
    all_to_all x2, starting transfers between devices, body(): lax.all_to_all(outgoing, 'shard', split_axis=0, concat_axis=0, tiled=True)  17.4 us
    dot_general x29, matrix products, mm(): lax.dot_general(a, b, (((ca,), (cb,)), ((), ())), preferred_element_type=...  14.3 us
    ppermute x4, starting transfers between devices, partner(): return lax.ppermute(value, axis, pairs)  9.69 us
  transfers between devices with their start and end apart: 11, of which 10 were waited for; matrix products, arithmetic and copies ran while one was open for 5% of the time, Pallas kernels for 0%

profile of v1, /device:TPU:14, one launch (start us, length us, event | category | flops | bytes accessed | tf_op | source)
XLA Modules:
  0.0 364.7 jit_solution(4682791775702241244)
XLA Ops:
  7.2 0.7 fusion.69
  8.1 1.5 convolution_convert_fusion.1
  9.6 1.3 copy.43
  10.9 17.3 %all-to-all-start = ((bf16[32,2,16,400]{3,2,1,0:T(8,128)(2,1)}), bf16[32,2,16,400]{3,2,1,0:T(8,128)(2,1)}, u32[]{:S(2)}, u32[]{:S(2)}) async-start(bf16[32,2,16,400]{3,2,1,0:T(8,128)(2,1)} %bitcast.3), calls=%async_computation | async-start | bytes 2097152 | tf_op jit(solution)/shard_map/all_to_all | solution.py:85
  28.2 2.9 copy.41
  31.2 1.2 gather_fusion
  32.9 47.7 %all-to-all-done = bf16[32,2,16,400]{3,2,1,0:T(8,128)(2,1)} async-done(((bf16[32,2,16,400]{3,2,1,0:T(8,128)(2,1)}), bf16[32,2,16,400]{3,2,1,0:T(8,128)(2,1)}, u32[]{:S(2)}, u32[]{:S(2)}) %all-to-all-start) | async-done | bytes 819232 | tf_op jit(solution)/shard_map/all_to_all | solution.py:85
  80.6 1.3 fusion.68
  81.9 1.9 collective-permute-start
  83.9 1.8 collective-permute-done
  88.9 2.0 collective-permute-start.1
  92.9 1.1 copy.46
  93.9 7.9 %all-to-all-start.1 = ((bf16[32,2,16,400]{3,2,1,0:T(8,128)(2,1)}), bf16[32,2,16,400]{3,2,1,0:T(8,128)(2,1)S(1)}, u32[]{:S(2)}, u32[]{:S(2)}) async-start(bf16[32,2,16,400]{3,2,1,0:T(8,128)(2,1)} %copy.46), calls=%async_computation.1 | async-start | bytes 2097152 | tf_op jit(solution)/shard_map/all_to_all | solution.py:100
  102.1 52.4 %all-to-all-done.1 = bf16[32,2,16,400]{3,2,1,0:T(8,128)(2,1)S(1)} async-done(((bf16[32,2,16,400]{3,2,1,0:T(8,128)(2,1)}), bf16[32,2,16,400]{3,2,1,0:T(8,128)(2,1)S(1)}, u32[]{:S(2)}, u32[]{:S(2)}) %all-to-all-start.1) | async-done | bytes 819232 | tf_op jit(solution)/shard_map/all_to_all | solution.py:100
  155.6 1.3 copy.48
  156.9 8.1 %all-to-all-start.2 = ((bf16[32,2,16,400]{3,2,1,0:T(8,128)(2,1)}), bf16[32,2,16,400]{3,2,1,0:T(8,128)(2,1)S(1)}, u32[]{:S(2)}, u32[]{:S(2)}) async-start(bf16[32,2,16,400]{3,2,1,0:T(8,128)(2,1)} %bitcast.13), calls=%async_computation.2 | async-start | bytes 2097152 | tf_op jit(solution)/shard_map/all_to_all | solution.py:85
  165.4 51.9 %all-to-all-done.2 = bf16[32,2,16,400]{3,2,1,0:T(8,128)(2,1)S(1)} async-done(((bf16[32,2,16,400]{3,2,1,0:T(8,128)(2,1)}), bf16[32,2,16,400]{3,2,1,0:T(8,128)(2,1)S(1)}, u32[]{:S(2)}, u32[]{:S(2)}) %all-to-all-start.2) | async-done | bytes 819232 | tf_op jit(solution)/shard_map/all_to_all | solution.py:85
  217.5 3.3 collective-permute-start.2
  220.8 10.8 %collective-permute-done.2 = bf16[512,400]{1,0:T(8,128)(2,1)S(1)} collective-permute-done((bf16[512,400]{1,0:T(8,128)(2,1)S(1)}, bf16[512,400]{1,0:T(8,128)(2,1)S(1)}, u32[]{:S(2)}, u32[]{:S(2)}) %collective-permute-start.2) | collective-permute-done | bytes 409632 | tf_op jit(solution)/shard_map/ppermute | solution.py:14
  235.1 5.7 %all-to-all-start.4 = ((s32[16,1,256]{2,1,0:T(1,128)}), s32[16,1,256]{2,1,0:T(1,128)S(1)}, u32[]{:S(2)}, u32[]{:S(2)}) async-start(s32[16,1,256]{2,1,0:T(1,128)} %stack.14), calls=%async_computation.4 | async-start | bytes 32768 | tf_op jit(solution)/shard_map/all_to_all | solution.py:108
  241.8 2.5 collective-permute-start.3
  245.4 16.6 %collective-permute-done.3 = bf16[512,400]{0,1:T(8,128)(2,1)S(1)} collective-permute-done((bf16[512,400]{0,1:T(8,128)(2,1)S(1)}, bf16[512,400]{0,1:T(8,128)(2,1)S(1)}, u32[]{:S(2)}, u32[]{:S(2)}) %collective-permute-start.3) | collective-permute-done | bytes 409632 | tf_op jit(solution)/shard_map/ppermute | solution.py:14
  262.3 1.1 copy.51
  263.4 9.4 %all-to-all-start.3 = ((bf16[32,2,16,400]{3,2,1,0:T(8,128)(2,1)}), bf16[32,2,16,400]{3,2,1,0:T(8,128)(2,1)S(1)}, u32[]{:S(2)}, u32[]{:S(2)}) async-start(bf16[32,2,16,400]{3,2,1,0:T(8,128)(2,1)} %copy.51), calls=%async_computation.3 | async-start | bytes 2097152 | tf_op jit(solution)/shard_map/all_to_all | solution.py:100
  272.9 7.5 %all-gather.2.cloned.1.call-done = bf16[4096,400]{0,1:T(8,128)(2,1)} async-done(((bf16[256,400]{0,1:T(8,128)(2,1)}), bf16[4096,400]{0,1:T(8,128)(2,1)}) %all-gather.2.cloned.1.call-update) | async-done | bytes 3276816 | tf_op jit(solution)/shard_map/all_gather | solution.py:110
  280.4 3.0 fusion
  283.5 1.3 reshape.130
  284.7 39.4 %all-to-all-done.3 = bf16[32,2,16,400]{3,2,1,0:T(8,128)(2,1)S(1)} async-done(((bf16[32,2,16,400]{3,2,1,0:T(8,128)(2,1)}), bf16[32,2,16,400]{3,2,1,0:T(8,128)(2,1)S(1)}, u32[]{:S(2)}, u32[]{:S(2)}) %all-to-all-start.3) | async-done | bytes 819232 | tf_op jit(solution)/shard_map/all_to_all | solution.py:100
  324.1 7.2 %all-to-all-start.5 = ((f32[32,1,2000]{2,1,0:T(1,128)}), f32[32,1,2000]{2,1,0:T(1,128)S(1)}, u32[]{:S(2)}, u32[]{:S(2)}) async-start(f32[32,1,2000]{2,1,0:T(1,128)} %reshape.130), calls=%async_computation.5 | async-start | bytes 524288 | tf_op jit(solution)/shard_map/all_to_all | solution.py:115
  332.4 0.8 divide_subtract_fusion
  333.1 21.2 %all-to-all-done.5 = f32[32,1,2000]{2,1,0:T(1,128)S(1)} async-done(((f32[32,1,2000]{2,1,0:T(1,128)}), f32[32,1,2000]{2,1,0:T(1,128)S(1)}, u32[]{:S(2)}, u32[]{:S(2)}) %all-to-all-start.5) | async-done | bytes 256032 | tf_op jit(solution)/shard_map/all_to_all | solution.py:115
  354.9 1.3 reduce
  (88 shorter events, 16.9 us)
Async XLA Ops:
  10.9 69.8 %all-to-all-start = ((bf16[32,2,16,400]{3,2,1,0:T(8,128)(2,1)}), bf16[32,2,16,400]{3,2,1,0:T(8,128)(2,1)}, u32[]{:S(2)}, u32[]{:S(2)}) async-start(bf16[32,2,16,400]{3,2,1,0:T(8,128)(2,1)} %bitcast.3), calls=%async_computation | async-start | bytes 2097152 | tf_op jit(solution)/shard_map/all_to_all | solution.py:85
  28.2 2.9 copy-start.1
  31.1 1.4 copy-start.2
  31.1 1.6 copy-start.3
  31.1 1.8 copy-start.4
  31.2 52.7 %copy-start.5 = (s32[2,128]{1,0:T(2,128)S(1)}, s32[2,128]{1,0:T(2,128)}, u32[]{:S(2)}) copy-start(s32[2,128]{1,0:T(2,128)} %param.15) | copy-start | bytes 3076
  81.9 3.8 %collective-permute-start = (bf16[512,400]{1,0:T(8,128)(2,1)S(1)}, bf16[512,400]{1,0:T(8,128)(2,1)S(1)}, u32[]{:S(2)}, u32[]{:S(2)}) collective-permute-start(bf16[512,400]{1,0:T(8,128)(2,1)S(1)} %bitcast.73), channel_id=1, source_target_pairs={{0,32},{32,0},{64,96},{96,64},{128,160},{160,128},{192,224},{224,1... | collective-permute-start | bytes 1228808 | tf_op jit(solution)/shard_map/ppermute | solution.py:14
  88.9 3.6 collective-permute-start.1
  92.8 62.1 %copy-start.6 = (f32[64]{0:T(128)S(1)}, f32[64]{0:T(128)}, u32[]{:S(2)}) copy-start(f32[64]{0:T(128)} %param.11) | copy-start | bytes 772
  92.9 62.2 %copy-start = (f32[64,400]{1,0:T(8,128)S(1)}, f32[64,400]{1,0:T(8,128)}, u32[]{:S(2)}) copy-start(f32[64,400]{1,0:T(8,128)} %param.10) | copy-start | bytes 307204
  93.9 60.5 %all-to-all-start.1 = ((bf16[32,2,16,400]{3,2,1,0:T(8,128)(2,1)}), bf16[32,2,16,400]{3,2,1,0:T(8,128)(2,1)S(1)}, u32[]{:S(2)}, u32[]{:S(2)}) async-start(bf16[32,2,16,400]{3,2,1,0:T(8,128)(2,1)} %copy.46), calls=%async_computation.1 | async-start | bytes 2097152 | tf_op jit(solution)/shard_map/all_to_all | solution.py:100
  156.9 60.5 %all-to-all-start.2 = ((bf16[32,2,16,400]{3,2,1,0:T(8,128)(2,1)}), bf16[32,2,16,400]{3,2,1,0:T(8,128)(2,1)S(1)}, u32[]{:S(2)}, u32[]{:S(2)}) async-start(bf16[32,2,16,400]{3,2,1,0:T(8,128)(2,1)} %bitcast.13), calls=%async_computation.2 | async-start | bytes 2097152 | tf_op jit(solution)/shard_map/all_to_all | solution.py:85
  165.0 115.3 %all-gather.2.cloned.1.call-start = ((), (), s32[]{:S(2)}) async-start(), calls=%async_computation.6 | async-start | bytes 3481600 | tf_op jit(solution)/shard_map/all_gather | solution.py:110
  217.5 14.1 %collective-permute-start.2 = (bf16[512,400]{1,0:T(8,128)(2,1)S(1)}, bf16[512,400]{1,0:T(8,128)(2,1)S(1)}, u32[]{:S(2)}, u32[]{:S(2)}) collective-permute-start(bf16[512,400]{1,0:T(8,128)(2,1)S(1)} %bitcast.74), channel_id=1, source_target_pairs={{0,64},{32,96},{64,0},{96,32},{128,192},{160,224},{192,128},{224,1... | collective-permute-start | bytes 1228808 | tf_op jit(solution)/shard_map/ppermute | solution.py:14
  235.1 28.3 %all-to-all-start.4 = ((s32[16,1,256]{2,1,0:T(1,128)}), s32[16,1,256]{2,1,0:T(1,128)S(1)}, u32[]{:S(2)}, u32[]{:S(2)}) async-start(s32[16,1,256]{2,1,0:T(1,128)} %stack.14), calls=%async_computation.4 | async-start | bytes 32768 | tf_op jit(solution)/shard_map/all_to_all | solution.py:108
  241.8 20.2 %collective-permute-start.3 = (bf16[512,400]{0,1:T(8,128)(2,1)S(1)}, bf16[512,400]{0,1:T(8,128)(2,1)S(1)}, u32[]{:S(2)}, u32[]{:S(2)}) collective-permute-start(bf16[512,400]{0,1:T(8,128)(2,1)S(1)} %fusion.5), channel_id=1, source_target_pairs={{0,64},{32,96},{64,0},{96,32},{128,192},{160,224},{192,128},{224,1... | collective-permute-start | bytes 1228808 | tf_op jit(solution)/shard_map/ppermute | solution.py:14
  263.4 60.7 %all-to-all-start.3 = ((bf16[32,2,16,400]{3,2,1,0:T(8,128)(2,1)}), bf16[32,2,16,400]{3,2,1,0:T(8,128)(2,1)S(1)}, u32[]{:S(2)}, u32[]{:S(2)}) async-start(bf16[32,2,16,400]{3,2,1,0:T(8,128)(2,1)} %copy.51), calls=%async_computation.3 | async-start | bytes 2097152 | tf_op jit(solution)/shard_map/all_to_all | solution.py:100
  283.5 73.2 %copy-start.7 = (f32[5]{0:T(128)S(1)}, f32[5]{0:T(128)}, u32[]{:S(2)}) copy-start(f32[5]{0:T(128)} %param.13) | copy-start | bytes 64
  324.1 30.2 %all-to-all-start.5 = ((f32[32,1,2000]{2,1,0:T(1,128)}), f32[32,1,2000]{2,1,0:T(1,128)S(1)}, u32[]{:S(2)}, u32[]{:S(2)}) async-start(f32[32,1,2000]{2,1,0:T(1,128)} %reshape.130), calls=%async_computation.5 | async-start | bytes 524288 | tf_op jit(solution)/shard_map/all_to_all | solution.py:115
Sparse Core Ops, SparseCore 0:
  234.6 45.7 all-gather.1
